TPU v7x, 32 devices: a whole 2x2x4 slice. The times are simulated.
32 devices in a mesh: dp: 8 (over y, x, core), seq: 4 (over z).
Axes of the slice: x: 2, y: 2, z: 4, core: 2. Of those that a mesh axis runs over, the one named last changes fastest.
Arguments:
- layer_input: bfloat16 [16, 512, 768], P('dp', 'seq'), may hold values from -6 to 6
- segment_ids: int32 [16, 512], P('dp', 'seq'), may hold values from 0 to 2, as said below
- w_query: bfloat16 [768, 768], replicated, may hold values from -0.21875 to 0.21875
- b_query: float32 [768], replicated, may hold values from -1.5 to 1.5
- w_key: bfloat16 [768, 768], replicated, may hold values from -0.21875 to 0.21875
- w_value: bfloat16 [768, 768], replicated, may hold values from -0.21875 to 0.21875
- b_value: float32 [768], replicated, may hold values from -1.5 to 1.5
- w_out: bfloat16 [768, 768], replicated, may hold values from -1.75 to 1.75
- b_out: float32 [768], replicated, may hold values from -1.5 to 1.5
- gain_one: float32 [768], replicated, may hold values from 0.5 to 1.5
- shift_one: float32 [768], replicated, may hold values from -1.5 to 1.5
- w_inner: bfloat16 [768, 3072], replicated, may hold values from -0.21875 to 0.21875
- b_inner: float32 [3072], replicated, may hold values from -1.5 to 1.5
- w_outer: bfloat16 [3072, 768], replicated, may hold values from -0.109375 to 0.109375
- b_outer: float32 [768], replicated, may hold values from -1.5 to 1.5
- gain_two: float32 [768], replicated, may hold values from 0.5 to 1.5
- shift_two: float32 [768], replicated, may hold values from -1.5 to 1.5
- cotangent: bfloat16 [16, 512, 768], P('dp', 'seq'), may hold values from -6 to 6
Outputs:
- output: bfloat16 [16, 512, 768], P('dp', 'seq')
- d_input: bfloat16 [16, 512, 768], P('dp', 'seq')
- d_w_query: float32 [768, 768], replicated
- d_b_query: float32 [768], replicated
- d_w_key: float32 [768, 768], replicated
- d_w_value: float32 [768, 768], replicated
- d_b_value: float32 [768], replicated
- d_w_out: float32 [768, 768], replicated
- d_b_out: float32 [768], replicated
- d_gain_one: float32 [768], replicated
- d_shift_one: float32 [768], replicated
- d_w_inner: float32 [768, 3072], replicated
- d_b_inner: float32 [3072], replicated
- d_w_outer: float32 [3072, 768], replicated
- d_b_outer: float32 [768], replicated
- d_gain_two: float32 [768], replicated
- d_shift_two: float32 [768], replicated
Inputs may be any that keep to these rules, and one draw needn't show every extreme that they name: `segment_ids`: each row holds either one pair (ids 1, then 0 for padding at its end) of more than 256 tokens, or two pairs packed in halves of 256 positions (ids 1 in the first half, 2 in the second, each followed by padding 0 in its half), each of 128 tokens or more. Some row is a single pair without padding, some row is packed with padding.
All inputs are finite; a program needn't handle non-finite values.
Results may differ from a plain program's by a relative error of at most 0.015.
Values may be sent and summed in bfloat16 or wider, within the bound.
A program may use at most 192 MiB of HBM per device.

v0:
```python
import math
import jax
import jax.numpy as jnp
from jax import lax
from jax.sharding import PartitionSpec as P

HD = 64
EPSILON = 1e-12
MASKED = -1000000000.0
INV_ROOT_TWO = 0.7071067811865476
DENSITY = 0.3989422804014327


def product(left, right):
    return jnp.dot(left, right, preferred_element_type=jnp.float32)


def product_tn(left, right):
    return lax.dot_general(
        left, right, (((0,), (0,)), ((), ())), preferred_element_type=jnp.float32
    )


def product_nt(left, right):
    return lax.dot_general(
        left, right, (((1,), (1,)), ((), ())), preferred_element_type=jnp.float32
    )


def layer_norm(values, scale_gain, offset):
    centre = values - jnp.mean(values, axis=-1, keepdims=True)
    inverse_std = lax.rsqrt(jnp.mean(centre * centre, axis=-1, keepdims=True) + EPSILON)
    normed = centre * inverse_std
    return (normed * scale_gain + offset, normed, inverse_std)


def norm_back(grad_out, normed, inverse_std, scale_gain):
    scaled = grad_out * scale_gain
    return inverse_std * (
        scaled
        - jnp.mean(scaled, axis=-1, keepdims=True)
        - normed * jnp.mean(scaled * normed, axis=-1, keepdims=True)
    )


def split_heads(tensor):
    return tensor.reshape(tensor.shape[0], tensor.shape[1], tensor.shape[2] // HD, HD)


def grouped(tensor, group):
    return tensor.reshape((tensor.shape[0] // group, group) + tensor.shape[1:])


def ungrouped(tensor):
    return tensor.reshape((tensor.shape[0] * tensor.shape[1],) + tensor.shape[2:])


def masked_scores(query_rows, key_rows, query_segs, key_segs):
    scores = (
        jnp.einsum(
            "rqhd,rkhd->rhqk",
            split_heads(query_rows),
            split_heads(key_rows),
            preferred_element_type=jnp.float32,
        )
        * 0.125
    )
    same_pair = query_segs[:, None, :, None] == key_segs[:, None, None, :]
    return jnp.where(same_pair, scores, MASKED)


def attend(packed_item):
    query_rows, key_rows, value_rows, query_segs, key_segs = packed_item
    scores = masked_scores(query_rows, key_rows, query_segs, key_segs)
    row_max = jnp.max(scores, axis=-1, keepdims=True)
    powers = jnp.exp(scores - row_max)
    totals = jnp.sum(powers, axis=-1, keepdims=True)
    soft_probs = (powers / totals).astype(jnp.bfloat16)
    attended = jnp.einsum(
        "rhqk,rkhd->rqhd", soft_probs, split_heads(value_rows), preferred_element_type=jnp.float32
    )
    return (attended.reshape(query_rows.shape), (row_max + jnp.log(totals))[..., 0])


def attend_back(packed_item):
    query_rows, key_rows, value_rows, query_segs, key_segs, log_total, grad_attn, attended = (
        packed_item
    )
    scores = masked_scores(query_rows, key_rows, query_segs, key_segs)
    probs = jnp.exp(scores - log_total[..., None])
    grad_heads = split_heads(grad_attn)
    delta = jnp.sum(grad_heads.astype(jnp.float32) * split_heads(attended), axis=-1)
    delta = jnp.swapaxes(delta, 1, 2)[..., None]
    grad_prob = jnp.einsum(
        "rqhd,rkhd->rhqk", grad_heads, split_heads(value_rows), preferred_element_type=jnp.float32
    )
    grad_scores = (probs * (grad_prob - delta)).astype(jnp.bfloat16)
    grad_query = (
        jnp.einsum(
            "rhqk,rkhd->rqhd",
            grad_scores,
            split_heads(key_rows),
            preferred_element_type=jnp.float32,
        )
        * 0.125
    )
    grad_keys = (
        jnp.einsum(
            "rhqk,rqhd->rkhd",
            grad_scores,
            split_heads(query_rows),
            preferred_element_type=jnp.float32,
        )
        * 0.125
    )
    grad_values = jnp.einsum(
        "rhqk,rqhd->rkhd",
        probs.astype(jnp.bfloat16),
        grad_heads,
        preferred_element_type=jnp.float32,
    )
    return (
        grad_query.reshape(query_rows.shape),
        grad_keys.reshape(key_rows.shape),
        grad_values.reshape(key_rows.shape),
    )


def on_device(
    layer_input,
    segment_ids,
    w_query,
    b_query,
    w_key,
    w_value,
    b_value,
    w_out,
    b_out,
    gain_one,
    shift_one,
    w_inner,
    b_inner,
    w_outer,
    b_outer,
    gain_two,
    shift_two,
    cotangent,
):
    row_count, shard_len, model_dim = layer_input.shape
    tok_count = row_count * shard_len
    tokens = layer_input.reshape(tok_count, model_dim)
    query_flat = (product(tokens, w_query) + b_query).astype(jnp.bfloat16)
    key_flat = product(tokens, w_key).astype(jnp.bfloat16)
    value_flat = (product(tokens, w_value) + b_value).astype(jnp.bfloat16)
    stacked = jnp.stack([key_flat, value_flat]).reshape(2, row_count, shard_len, model_dim)
    context, seg_context = (
        lax.all_gather(stacked, "seq", axis=2, tiled=True),
        lax.all_gather(segment_ids, "seq", axis=1, tiled=True),
    )
    group = math.gcd(row_count, max(1, 512 // shard_len))
    query_grid = grouped(query_flat.reshape(row_count, shard_len, model_dim), group)
    query_segs = grouped(segment_ids, group)
    key_segs = grouped(seg_context, group)
    attn_grid, log_total = lax.map(
        attend,
        (query_grid, grouped(context[0], group), grouped(context[1], group), query_segs, key_segs),
    )
    attn_low = ungrouped(attn_grid).reshape(tok_count, model_dim).astype(jnp.bfloat16)
    branch = product(attn_low, w_out) + b_out
    hidden_one, normed_one, inverse_one = layer_norm(
        tokens.astype(jnp.float32) + branch, gain_one, shift_one
    )
    hidden_low = hidden_one.astype(jnp.bfloat16)
    inner_pre = product(hidden_low, w_inner) + b_inner
    cdf_part = 0.5 * (1.0 + lax.erf(inner_pre * INV_ROOT_TWO))
    active_low = (inner_pre * cdf_part).astype(jnp.bfloat16)
    outer_out = product(active_low, w_outer) + b_outer
    result, normed_two, inverse_two = layer_norm(hidden_one + outer_out, gain_two, shift_two)
    grad_out = cotangent.reshape(tok_count, model_dim).astype(jnp.float32)
    grad_gain_two = jnp.sum(grad_out * normed_two, axis=0)
    grad_shift_two = jnp.sum(grad_out, axis=0)
    grad_two = norm_back(grad_out, normed_two, inverse_two, gain_two)
    grad_outer = grad_two.astype(jnp.bfloat16)
    grad_w_outer = product_tn(active_low, grad_outer)
    grad_b_outer = jnp.sum(grad_outer.astype(jnp.float32), axis=0)
    grad_active = product_nt(grad_outer, w_outer)
    slope = cdf_part + inner_pre * DENSITY * jnp.exp(-0.5 * inner_pre * inner_pre)
    grad_inner = (grad_active * slope).astype(jnp.bfloat16)
    grad_w_inner = product_tn(hidden_low, grad_inner)
    grad_b_inner = jnp.sum(grad_inner.astype(jnp.float32), axis=0)
    grad_hidden = grad_two + product_nt(grad_inner, w_inner)
    grad_gain_one = jnp.sum(grad_hidden * normed_one, axis=0)
    grad_shift_one = jnp.sum(grad_hidden, axis=0)
    grad_one = norm_back(grad_hidden, normed_one, inverse_one, gain_one)
    grad_branch = grad_one.astype(jnp.bfloat16)
    grad_w_out = product_tn(attn_low, grad_branch)
    grad_b_out = jnp.sum(grad_branch.astype(jnp.float32), axis=0)
    grad_attn = product_nt(grad_branch, w_out).astype(jnp.bfloat16)
    grad_attn_grid = grouped(grad_attn.reshape(row_count, shard_len, model_dim), group)
    query_part, key_part, value_part = lax.map(
        attend_back,
        (
            query_grid,
            grouped(context[0], group),
            grouped(context[1], group),
            query_segs,
            key_segs,
            log_total,
            grad_attn_grid,
            attn_grid,
        ),
    )
    key_home, value_home = (
        lax.psum_scatter(
            ungrouped(key_part).astype(jnp.bfloat16), "seq", scatter_dimension=1, tiled=True
        ).astype(jnp.float32),
        lax.psum_scatter(
            ungrouped(value_part).astype(jnp.bfloat16), "seq", scatter_dimension=1, tiled=True
        ).astype(jnp.float32),
    )
    grad_query = ungrouped(query_part).reshape(tok_count, model_dim).astype(jnp.bfloat16)
    grad_key = key_home.reshape(tok_count, model_dim).astype(jnp.bfloat16)
    grad_value = value_home.reshape(tok_count, model_dim).astype(jnp.bfloat16)
    grad_w_query = product_tn(tokens, grad_query)
    grad_b_query = jnp.sum(grad_query.astype(jnp.float32), axis=0)
    grad_w_key = product_tn(tokens, grad_key)
    grad_w_value = product_tn(tokens, grad_value)
    grad_b_value = jnp.sum(grad_value.astype(jnp.float32), axis=0)
    grad_input = (
        grad_one
        + product_nt(grad_query, w_query)
        + product_nt(grad_key, w_key)
        + product_nt(grad_value, w_value)
    )
    summed = lax.psum(
        (
            grad_w_query,
            grad_b_query,
            grad_w_key,
            grad_w_value,
            grad_b_value,
            grad_w_out,
            grad_b_out,
            grad_w_outer,
            grad_b_outer,
            grad_gain_two,
            grad_shift_two,
            grad_w_inner,
            grad_b_inner,
            grad_gain_one,
            grad_shift_one,
        ),
        ("dp", "seq"),
    )
    return (
        result.reshape(row_count, shard_len, model_dim).astype(jnp.bfloat16),
        grad_input.reshape(row_count, shard_len, model_dim).astype(jnp.bfloat16),
        summed[0],
        summed[1],
        summed[2],
        summed[3],
        summed[4],
        summed[5],
        summed[6],
        summed[13],
        summed[14],
        summed[11],
        summed[12],
        summed[7],
        summed[8],
        summed[9],
        summed[10],
    )


def solution(mesh):
    return jax.shard_map(
        on_device,
        mesh=mesh,
        in_specs=(
            P("dp", "seq", None),
            P("dp", "seq"),
            P(),
            P(),
            P(),
            P(),
            P(),
            P(),
            P(),
            P(),
            P(),
            P(),
            P(),
            P(),
            P(),
            P(),
            P(),
            P("dp", "seq", None),
        ),
        out_specs=(
            P("dp", "seq", None),
            P("dp", "seq", None),
            P(),
            P(),
            P(),
            P(),
            P(),
            P(),
            P(),
            P(),
            P(),
            P(),
            P(),
            P(),
            P(),
            P(),
            P(),
        ),
        check_vma=False,
    )
```

profile of v0, /device:TPU:0, one launch (start us, length us, event | category | flops | bytes accessed | tf_op | source)
XLA Modules:
  0.0 666.1 jit_solution(12733375049098746954)
XLA Ops:
  14.2 12.6 %all_gather.7 = s32[2,512]{1,0:T(2,128)S(1)} all-gather(s32[2,128]{1,0:T(2,128)S(1)} %copy-done.40), channel_id=1, replica_groups=mesh['dp'=8,'seq'=4] {'seq'}, dimensions={1}, use_global_device_ids=true | all-gather | bytes 5120 | tf_op jit(solution)/shard_map/all_gather | solution.py:158
  28.3 50.1 %all-gather.2.cloned.1.call-done = bf16[2,2,512,768]{3,2,1,0:T(8,128)(2,1)} async-done(((bf16[2,2,128,768]{3,2,1,0:T(8,128)(2,1)}), bf16[2,2,512,768]{3,2,1,0:T(8,128)(2,1)}) %all-gather.2.cloned.1.call-update) | async-done | bytes 3145744 | tf_op jit(solution)/shard_map/all_gather | solution.py:157
  78.4 3.7 fusion.60
  83.9 2.6 copy.42
  86.5 2.3 fusion.3
  91.5 3.1 fusion.61
  102.4 3.0 convert_reduce_fusion
  112.3 4.6 multiply_convert_fusion
  120.3 2.6 copy.52
  123.0 5.5 fusion.14
  128.5 2.6 copy.54
  131.2 3.2 convert_reduce_fusion.5
  138.6 5.2 fusion.49
  143.8 5.3 fusion.56
  149.2 7.9 %reduce-scatter.3.cloned.1.call-done = bf16[2,128,768]{2,1,0:T(8,128)(2,1)} async-done(((bf16[2,512,768]{2,1,0:T(8,128)(2,1)}), bf16[2,128,768]{2,1,0:T(8,128)(2,1)}) %reduce-scatter.3.cloned.1.call-update) | async-done | bytes 393232 | tf_op jit(solution)/shard_map/reduce_scatter | solution.py:214
  157.0 2.9 convolution_bitcast_fusion.1
  160.0 34.3 %reduce-scatter.5.cloned.1.call-done = bf16[2,128,768]{2,1,0:T(8,128)(2,1)} async-done(((bf16[2,512,768]{2,1,0:T(8,128)(2,1)}), bf16[2,128,768]{2,1,0:T(8,128)(2,1)}) %reduce-scatter.5.cloned.1.call-update) | async-done | bytes 393232 | tf_op jit(solution)/shard_map/reduce_scatter | solution.py:217
  194.2 2.9 convolution_bitcast_fusion
  199.8 42.9 %all-reduce = (f32[768]{0:T(1024)}, f32[768]{0:T(1024)}, f32[768]{0:T(1024)}, f32[768]{0:T(1024)}, f32[768]{0:T(1024)}, /*index=5*/f32[3072]{0:T(1024)}, f32[768]{0:T(1024)}, f32[768]{0:T(1024)}, f32[768]{0:T(1024)}) all-reduce(f32[768]{0:T(1024)S(1)} %copy-done.36, ...), channel_id=1, replica_groups=mesh['dp'=8,'seq'=4] {'dp','seq'}, use_global_device_ids=true, to_apply=%region_15.16 | all-reduce | flops 9216 | bytes 73728 | tf_op jit(solution)/shard_map/psum | solution.py:235
  245.6 391.2 %all-reduce.4.cloned.1.call-done = (f32[768,768]{0,1:T(8,128)}, f32[768,768]{0,1:T(8,128)}, f32[768,768]{0,1:T(8,128)}, f32[768,768]{1,0:T(8,128)}, f32[768,3072]{1,0:T(8,128)}, /*index=5*/f32[3072,768]{1,0:T(8,128)}) async-done(((f32[768,768]{0,1:T(8,128)}, f32[768,768]{0,1:T(8,128)}, f32[768,768]{0,1:T(8,128)}, f32[768,768]{1,0:T(8,128)}, f32[768,3072]{1,0:T(8,128)}, /*index=5*/f32[3072,768]{1,0:T(8,128)}), ...) | async-done | bytes 28311568 | tf_op jit(solution)/shard_map/psum | solution.py:235
  636.7 3.2 copy.57
  641.9 3.2 copy.59
  646.5 9.3 %copy.100 = f32[768,3072]{1,0:T(8,128)} copy(f32[768,3072]{1,0:T(8,128)} %get-tuple-element.169) | data formatting | bytes 18874368
  655.8 3.7 copy.101
  (158 shorter events, 43.8 us)
Async XLA Ops:
  7.2 87.9 %copy-start = (bf16[768,768]{1,0:T(8,128)(2,1)S(1)}, bf16[768,768]{1,0:T(8,128)(2,1)}, u32[]{:S(2)}) copy-start(bf16[768,768]{1,0:T(8,128)(2,1)} %param.25) | copy-start | bytes 3538948
  7.2 71.2 %all-gather.2.cloned.1.call-start = ((), (), s32[]{:S(2)}) async-start(), calls=%async_computation.2 | async-start | bytes 3932160 | tf_op jit(solution)/shard_map/all_gather | solution.py:157
  7.3 4.9 copy-start.6
  7.3 4.9 copy-start.42
  11.1 15.7 %copy-start.11 = (bf16[2,128,768]{2,1,0:T(8,128)(2,1)S(1)}, bf16[2,128,768]{2,1,0:T(8,128)(2,1)}, u32[]{:S(2)}) copy-start(bf16[2,128,768]{2,1,0:T(8,128)(2,1)} %param.35) | copy-start | bytes 1179652
  11.1 15.7 %copy-start.30 = (f32[768]{0:T(1024)S(1)}, f32[768]{0:T(1024)}, u32[]{:S(2)}) copy-start(f32[768]{0:T(1024)} %param.33) | copy-start | bytes 9220
  12.1 144.9 %reduce-scatter.3.cloned.1.call-start = ((), (), s32[]{:S(2)}) async-start(), calls=%async_computation.3 | async-start | bytes 1966080 | tf_op jit(solution)/shard_map/reduce_scatter | solution.py:214
  14.2 72.3 %copy-start.9 = (bf16[2,128,12,64]{1,0,3,2:T(2,128)(2,1)}, bf16[2,128,12,64]{1,0,3,2:T(2,128)(2,1)S(1)}, u32[]{:S(2)}) copy-start(bf16[2,128,12,64]{1,0,3,2:T(2,128)(2,1)S(1)} %reshape.206) | copy-start | bytes 1179652
  91.4 4.5 slice-start.5
  91.5 4.5 slice-start.6
  95.7 11.9 %copy-start.4 = (f32[256,768]{1,0:T(8,128)}, f32[256,768]{1,0:T(8,128)S(1)}, u32[]{:S(2)}) copy-start(f32[256,768]{1,0:T(8,128)S(1)} %get-tuple-element.146) | copy-start | bytes 2359300
  95.7 11.9 %copy-start.31 = (f32[256]{0:T(256)}, f32[256]{0:T(256)S(1)}, u32[]{:S(2)}) copy-start(f32[256]{0:T(256)S(1)} %broadcast_multiply_fusion.4) | copy-start | bytes 3076
  96.0 11.6 %copy-start.37 = (f32[256]{0:T(256)}, f32[256]{0:T(256)S(1)}, u32[]{:S(2)}) copy-start(f32[256]{0:T(256)S(1)} %add_rsqrt_fusion.1) | copy-start | bytes 3076
  112.3 6.3 copy-start.10
  122.9 71.3 %reduce-scatter.5.cloned.1.call-start = ((), (), s32[]{:S(2)}) async-start(), calls=%async_computation.4 | async-start | bytes 1966080 | tf_op jit(solution)/shard_map/reduce_scatter | solution.py:217
  131.1 505.6 %all-reduce.4.cloned.1.call-start = ((), (), s32[]{:S(2)}) async-start(), calls=%async_computation.5 | async-start | bytes 56623104 | tf_op jit(solution)/shard_map/psum | solution.py:235
  138.6 5.2 copy-start.5
  138.6 5.2 copy-start.24
  138.6 5.2 copy-start.32
  138.6 5.2 copy-start.38
  197.2 45.5 %copy-start.8 = (bf16[768,768]{1,0:T(8,128)(2,1)S(1)}, bf16[768,768]{1,0:T(8,128)(2,1)}, u32[]{:S(2)}) copy-start(bf16[768,768]{1,0:T(8,128)(2,1)} %param.22) | copy-start | bytes 3538948
  645.1 10.7 %slice-start = ((s8[9437184]{0:T(1024)(128)(4,1)}), s8[4194304]{0:T(1024)(128)(4,1)S(1)}, s32[]{:S(2)}) async-start(s8[9437184]{0:T(1024)(128)(4,1)} %bitcast.106), calls=%async_computation.6 | async-start | bytes 8388608
  646.5 9.3 %slice-start.1 = ((s8[9437184]{0:T(1024)(128)(4,1)}), s8[4194304]{0:T(1024)(128)(4,1)S(1)}, s32[]{:S(2)}) async-start(s8[9437184]{0:T(1024)(128)(4,1)} %bitcast.106), calls=%async_computation.7 | async-start | bytes 8388608
  646.5 9.3 %slice-start.2 = ((s8[9437184]{0:T(1024)(128)(4,1)}), s8[1048576]{0:T(1024)(128)(4,1)S(1)}, s32[]{:S(2)}) async-start(s8[9437184]{0:T(1024)(128)(4,1)} %bitcast.106), calls=%async_computation.8 | async-start | bytes 2097152
  (32 other events, 79.5 us)
Sparse Core Ops, SparseCore 0:
  12.2 66.1 all-gather.1
  123.0 33.9 reduce-scatter.2
  159.9 34.2 reduce-scatter.4
  201.6 435.0 all-reduce.3
where the time goes:
time: 667 us; the launch traced here: 666 us
  waiting for transfers between devices  483 us (72%)
  matrix products  61.2 us (9%)
  blocking collectives  55.5 us (8%)
  local copies, waits for them, and re-layouts  41 us (6%)
  between operations  14.4 us (2%)
  other arithmetic  10.4 us (2%)
    psum x1, waiting for transfers between devices, on_device(): lax.psum((grad_w_query, grad_b_query, grad_w_key, grad_w_value, grad_b_va...  391 us
    all_gather x1, waiting for transfers between devices, on_device(): lax.all_gather(stacked, 'seq', axis=2, tiled=True)  50.1 us
    psum x1, blocking collectives, on_device(): lax.psum((grad_w_query, grad_b_query, grad_w_key, grad_w_value, grad_b_va...  42.9 us
    reduce_scatter x1, waiting for transfers between devices, on_device(): lax.psum_scatter(ungrouped(value_part).astype(jnp.bfloat16), 'seq', scatt...  34.3 us
    unnamed x110, local copies, waits for them, and re-layouts  24.8 us
    dot_general x6, matrix products, product_tn(): lax.dot_general(left, right, (((0,), (0,)), ((), ())), preferred_element_...  20.1 us
  transfers between devices with their start and end apart: 4, of which 4 were waited for; matrix products, arithmetic and copies ran while one was open for 6% of the time, Pallas kernels for 0%

commit v1 on v0

--- a/solution.py
+++ b/solution.py
@@ -232,7 +232,7 @@
         + product_nt(grad_key, w_key)
         + product_nt(grad_value, w_value)
     )
-    summed = lax.psum(
+    one_axis = lax.psum(
         (
             grad_w_query,
             grad_b_query,
@@ -250,8 +250,9 @@
             grad_gain_one,
             grad_shift_one,
         ),
-        ("dp", "seq"),
-    )
+        "seq",
+    )
+    summed = lax.psum(one_axis, "dp")
     return (
         result.reshape(row_count, shard_len, model_dim).astype(jnp.bfloat16),
         grad_input.reshape(row_count, shard_len, model_dim).astype(jnp.bfloat16),

time: 667 us -> 1520 us (2.28)
  waiting for transfers between devices: 483 us -> 1340 us
    psum x1, waiting for transfers between devices: 391 us -> 941 us  [on_device(): lax.psum((grad_w_query, grad_b_query, grad_w_key, grad_w_value, grad_b_va...]
    psum x0 -> x1, waiting for transfers between devices: none -> 301 us  [on_device(): summed = lax.psum(one_axis, 'dp')]
    psum x0 -> x1, blocking collectives: none -> 25.9 us  [on_device(): summed = lax.psum(one_axis, 'dp')]
    psum x1, blocking collectives: 42.9 us -> 18.1 us  [on_device(): lax.psum((grad_w_query, grad_b_query, grad_w_key, grad_w_value, grad_b_va...]
  transfers between devices with their start and end apart: 4 -> 5, of which waited for: 4 -> 5; matrix products, arithmetic and copies ran while one was open for 6% -> 2% of each run, Pallas kernels for 0% -> 0%
where the time goes in v1:
time: 1520 us
  waiting for transfers between devices  1340 us (88%)
  matrix products  59.9 us (4%)
  blocking collectives  56.5 us (4%)
  local copies, waits for them, and re-layouts  41 us (3%)
    psum x1, waiting for transfers between devices, on_device(): lax.psum((grad_w_query, grad_b_query, grad_w_key, grad_w_value, grad_b_va...  941 us
    psum x1, waiting for transfers between devices, on_device(): summed = lax.psum(one_axis, 'dp')  301 us
    all_gather x1, waiting for transfers between devices, on_device(): lax.all_gather(stacked, 'seq', axis=2, tiled=True)  51.3 us
    reduce_scatter x1, waiting for transfers between devices, on_device(): lax.psum_scatter(ungrouped(value_part).astype(jnp.bfloat16), 'seq', scatt...  34.3 us
  transfers between devices with their start and end apart: 5, of which 5 were waited for; matrix products, arithmetic and copies ran while one was open for 2% of the time, Pallas kernels for 0%

profile of v1, /device:TPU:0, one launch (start us, length us, event | category | flops | bytes accessed | tf_op | source)
XLA Modules:
  0.0 1518.0 jit_solution(1093609214717297814)
XLA Ops:
  13.0 12.6 all_gather.7
  27.1 51.3 %all-gather.2.cloned.1.call-done = bf16[2,2,512,768]{3,2,1,0:T(8,128)(2,1)} async-done(((bf16[2,2,128,768]{3,2,1,0:T(8,128)(2,1)}), bf16[2,2,512,768]{3,2,1,0:T(8,128)(2,1)}) %all-gather.2.cloned.1.call-update) | async-done | bytes 3145744 | tf_op jit(solution)/shard_map/all_gather | solution.py:157
  78.5 3.7 fusion.60
  83.9 2.6 copy.42
  91.5 3.1 fusion.61
  102.4 3.0 convert_reduce_fusion
  112.3 4.6 multiply_convert_fusion
  120.3 2.6 copy.52
  123.0 5.5 fusion.14
  131.2 3.2 convert_reduce_fusion.5
  138.7 5.2 fusion.49
  143.9 5.3 fusion.56
  149.2 7.9 reduce-scatter.3.cloned.1.call-done
  157.1 2.9 convolution_bitcast_fusion.1
  160.0 34.3 %reduce-scatter.5.cloned.1.call-done = bf16[2,128,768]{2,1,0:T(8,128)(2,1)} async-done(((bf16[2,512,768]{2,1,0:T(8,128)(2,1)}), bf16[2,128,768]{2,1,0:T(8,128)(2,1)}) %reduce-scatter.5.cloned.1.call-update) | async-done | bytes 393232 | tf_op jit(solution)/shard_map/reduce_scatter | solution.py:217
  194.3 2.9 convolution_bitcast_fusion
  197.3 940.9 %all-reduce.9.cloned.1.call-done = (f32[768,768]{0,1:T(8,128)}, f32[768,768]{0,1:T(8,128)}, f32[768,768]{0,1:T(8,128)}, f32[768,768]{1,0:T(8,128)}, f32[768,3072]{1,0:T(8,128)}, /*index=5*/f32[3072,768]{1,0:T(8,128)}) async-done(((f32[768,768]{0,1:T(8,128)}, f32[768,768]{0,1:T(8,128)}, f32[768,768]{0,1:T(8,128)}, f32[768,768]{1,0:T(8,128)}, f32[768,3072]{1,0:T(8,128)}, /*index=5*/f32[3072,768]{1,0:T(8,128)}), ...) | async-done | bytes 28311568 | tf_op jit(solution)/shard_map/psum | solution.py:235
  1140.8 18.1 %all-reduce.2 = (f32[768]{0:T(1024)S(1)}, f32[768]{0:T(1024)S(1)}, f32[768]{0:T(1024)S(1)}, f32[768]{0:T(1024)S(1)}, f32[768]{0:T(1024)S(1)}, /*index=5*/f32[307...) all-reduce(f32[768]{0:T(1024)S(1)} %copy-done.37, ...), channel_id=1, replica_groups=mesh['dp'=8,'seq'=4] {'seq'}, use_global_device_ids=true, to_apply=%region_16.17 | all-reduce | flops 9216 | bytes 73728 | tf_op jit(solution)/shard_map/psum | solution.py:235
  1158.9 25.9 %all-reduce = (f32[768]{0:T(1024)}, f32[768]{0:T(1024)}, f32[768]{0:T(1024)}, f32[768]{0:T(1024)}, f32[768]{0:T(1024)}, /*index=5*/f32[3072]{0:T(1024)}, f32[768]{0:T(1024)}, f32[768]{0:T(1024)}, f32[768]{0:T(1024)}) all-reduce(f32[768]{0:T(1024)S(1)} %get-tuple-element.134, ...), channel_id=1, replica_groups=mesh['dp'=8,'seq'=4] {'dp'}, use_global_device_ids=true, to_apply=%region_17.18 | all-reduce | flops 9216 | bytes 73728 | tf_op jit(solution)/shard_map/psum | solution.py:255
  1187.6 301.0 %all-reduce.7.cloned.1.call-done = (f32[768,768]{0,1:T(8,128)}, f32[768,768]{0,1:T(8,128)}, f32[768,768]{0,1:T(8,128)}, f32[768,768]{1,0:T(8,128)}, f32[768,3072]{1,0:T(8,128)}, /*index=5*/f32[3072,768]{1,0:T(8,128)}) async-done(((f32[768,768]{0,1:T(8,128)}, f32[768,768]{0,1:T(8,128)}, f32[768,768]{0,1:T(8,128)}, f32[768,768]{1,0:T(8,128)}, f32[768,3072]{1,0:T(8,128)}, /*index=5*/f32[3072,768]{1,0:T(8,128)}), ...) | async-done | bytes 28311568 | tf_op jit(solution)/shard_map/psum | solution.py:255
  1488.6 3.2 copy.57
  1493.7 3.2 copy.59
  1498.3 9.3 copy.106
  1507.7 3.7 copy.107
  (164 shorter events, 47.4 us)
Async XLA Ops:
  7.2 87.9 %copy-start = (bf16[768,768]{1,0:T(8,128)(2,1)S(1)}, bf16[768,768]{1,0:T(8,128)(2,1)}, u32[]{:S(2)}) copy-start(bf16[768,768]{1,0:T(8,128)(2,1)} %param.25) | copy-start | bytes 3538948
  7.2 71.3 %all-gather.2.cloned.1.call-start = ((), (), s32[]{:S(2)}) async-start(), calls=%async_computation.2 | async-start | bytes 3932160 | tf_op jit(solution)/shard_map/all_gather | solution.py:157
  7.3 5.0 copy-start.6
  7.3 5.0 copy-start.27
  7.3 5.0 copy-start.43
  11.2 14.5 copy-start.11
  11.2 14.5 copy-start.31
  12.2 144.9 %reduce-scatter.3.cloned.1.call-start = ((), (), s32[]{:S(2)}) async-start(), calls=%async_computation.3 | async-start | bytes 1966080 | tf_op jit(solution)/shard_map/reduce_scatter | solution.py:214
  13.0 73.5 %copy-start.9 = (bf16[2,128,12,64]{1,0,3,2:T(2,128)(2,1)}, bf16[2,128,12,64]{1,0,3,2:T(2,128)(2,1)S(1)}, u32[]{:S(2)}) copy-start(bf16[2,128,12,64]{1,0,3,2:T(2,128)(2,1)S(1)} %reshape.206) | copy-start | bytes 1179652
  95.7 11.9 copy-start.4
  95.7 11.9 copy-start.32
  96.0 11.6 copy-start.38
  112.3 6.3 copy-start.10
  123.0 71.3 %reduce-scatter.5.cloned.1.call-start = ((), (), s32[]{:S(2)}) async-start(), calls=%async_computation.4 | async-start | bytes 1966080 | tf_op jit(solution)/shard_map/reduce_scatter | solution.py:217
  131.2 1007.0 %all-reduce.9.cloned.1.call-start = ((), (), s32[]{:S(2)}) async-start(), calls=%async_computation.6 | async-start | bytes 56623104 | tf_op jit(solution)/shard_map/psum | solution.py:235
  138.7 5.2 copy-start.5
  138.7 5.2 copy-start.24
  138.7 5.2 copy-start.33
  138.7 5.2 copy-start.39
  197.2 1291.4 %all-reduce.7.cloned.1.call-start = ((), (), s32[]{:S(2)}) async-start(), calls=%async_computation.5 | async-start | bytes 56623104 | tf_op jit(solution)/shard_map/psum | solution.py:255
  1138.2 46.5 %copy-start.8 = (bf16[768,768]{1,0:T(8,128)(2,1)S(1)}, bf16[768,768]{1,0:T(8,128)(2,1)}, u32[]{:S(2)}) copy-start(bf16[768,768]{1,0:T(8,128)(2,1)} %param.22) | copy-start | bytes 3538948
  1496.9 10.7 slice-start
  1498.3 9.3 slice-start.1
  1498.3 9.3 slice-start.2
  (34 other events, 89.0 us)
Sparse Core Ops, SparseCore 0:
  12.3 66.1 all-gather.1
  123.1 33.9 reduce-scatter.2
  160.0 34.2 reduce-scatter.4
  198.6 939.5 all-reduce.8
  1143.6 344.9 all-reduce.6
